TPU v7x, 256 devices: a whole 4x4x8 slice. The times are simulated.
256 devices in a mesh: row: 32 (over z, x_lo, core), col: 8 (over y, x_hi).
Axes of the slice: x: 4 (x_hi: 2, x_lo: 2; x = x_hi * 2 + x_lo), y: 4, z: 8, core: 2. Of those that a mesh axis runs over, the one named last changes fastest.
Arguments:
- vectors: bfloat16 [8, 262144], P(None, ('row', 'col')), may hold values from -6 to 6
- energies: float32 [262144], P(('row', 'col')), may hold values from 0.5 to 6
- tiles: bfloat16 [262144, 4096], P(('row', 'col')), may hold values from -0.25 to 0.25
- tile_rows: int32 [262144], P(('row', 'col')), may hold values from 0 to 127, as said below
- tile_cols: int32 [262144], P(('row', 'col')), may hold values from 0 to 511
- tile_count: int32 [256], P(('row', 'col')), may hold values from 128 to 1024, as said below
Outputs:
- product: bfloat16 [8, 262144], P(None, ('row', 'col'))
- residual: float32 [8, 262144], P(None, ('row', 'col'))
Inputs may be any that keep to these rules, and one draw needn't show every extreme that they name: `tile_count`: every count is at least 128, and some device uses all 1024 slots in every draw; a few devices are full while most use far fewer. `tile_rows`: slots may name the same row and column block more than once; such tiles add.
All inputs are finite; a program needn't handle non-finite values.
Results may differ from a plain program's by a relative error of at most 0.008.
Values may be sent and summed in bfloat16 or wider, within the bound.
A program may use at most 64 MiB of HBM per device.

v0:
```python
import jax
import jax.numpy as jnp
from jax import lax
from jax.sharding import PartitionSpec as P


def per_device(vectors, energies, tiles, tile_rows, tile_cols, tile_count):
    kvec = vectors.shape[0]
    own_states = vectors.shape[1]
    blk_own = own_states // 64
    n_row = lax.axis_size("row")
    n_col = lax.axis_size("col")
    seg_blocks = n_col * blk_own
    slots = tiles.shape[0]
    group = min(128, slots)
    gathered = lax.all_gather(vectors, "row", axis=1, tiled=True)
    blocks = gathered.reshape(kvec, n_row * blk_own, 64)
    seg_ids = jnp.arange(seg_blocks, dtype=jnp.int32)
    group_ids = jnp.arange(group, dtype=jnp.int32)
    count = tile_count[0]
    turns = (count + group - 1) // group

    def add_group(step, accum):
        first = step * group
        tile_part = lax.dynamic_slice_in_dim(tiles, first, group, 0).reshape(group, 64, 64)
        row_part = lax.dynamic_slice_in_dim(tile_rows, first, group, 0)
        col_part = lax.dynamic_slice_in_dim(tile_cols, first, group, 0)
        picked = jnp.take(blocks, col_part, axis=1)
        prod = jnp.einsum("tji,kti->ktj", tile_part, picked, preferred_element_type=jnp.float32)
        live = first + group_ids < count
        onehot = ((row_part[:, None] == seg_ids[None, :]) & live[:, None]).astype(jnp.bfloat16)
        upper = prod.astype(jnp.bfloat16)
        lower = (prod - upper.astype(jnp.float32)).astype(jnp.bfloat16)
        added = jnp.einsum("ktj,tr->krj", upper, onehot, preferred_element_type=jnp.float32)
        added = added + jnp.einsum("ktj,tr->krj", lower, onehot, preferred_element_type=jnp.float32)
        return accum + added

    accum = jnp.zeros((kvec, seg_blocks, 64), jnp.float32)
    accum = lax.fori_loop(0, turns, add_group, accum)
    partial_value = accum.reshape(kvec, seg_blocks * 64)
    summed = lax.psum(partial_value.astype(jnp.bfloat16), "col").astype(jnp.float32)
    share = lax.dynamic_slice_in_dim(summed, lax.axis_index("col") * own_states, own_states, 1)
    vec32 = vectors.astype(jnp.float32)
    diag_part = energies[None, :] * vec32
    whole = diag_part + share
    terms = jnp.einsum("an,bn->ab", vec32, whole, precision=lax.Precision.HIGHEST)
    total_states = n_row * n_col * own_states
    gram = lax.psum(terms, ("row", "col")) / total_states
    residual = whole - jnp.einsum("ab,an->bn", gram, vec32, precision=lax.Precision.HIGHEST)
    return (whole.astype(jnp.bfloat16), residual)


def solution(mesh):
    in_specs = (
        P(None, ("row", "col")),
        P(("row", "col")),
        P(("row", "col"), None),
        P(("row", "col")),
        P(("row", "col")),
        P(("row", "col")),
    )
    out_specs = (P(None, ("row", "col")), P(None, ("row", "col")))
    return jax.shard_map(
        per_device, mesh=mesh, in_specs=in_specs, out_specs=out_specs, check_vma=False
    )
```

profile of v0, /device:TPU:1, one launch (start us, length us, event | category | flops | bytes accessed | tf_op | source)
XLA Modules:
  0.0 307.5 jit_solution(10586212366115992367)
XLA Ops:
  7.9 40.2 %all_gather.3 = bf16[8,32768]{1,0:T(8,128)(2,1)S(1)} all-gather(bf16[8,1024]{1,0:T(8,128)(2,1)} %param.8), channel_id=1, replica_groups=mesh['row'=32,'col'=8] {'row'}, dimensions={1}, use_global_device_ids=true | all-gather | bytes 540672 | tf_op jit(solution)/shard_map/all_gather | solution.py:16
  48.0 1.1 reshape.25
  49.2 1.7 copy.20
  50.9 22.4 %while.13 = (s32[]{:T(128)}, f32[8,128,64]{1,2,0:T(8,128)S(1)}, s32[]{:T(128)}, s32[1024]{0:T(1024)}, s32[]{:T(128)}, /*index=5*/s32[1024]{0:T(1024)}, bf16[8,51...) while((s32[]{:T(128)}, f32[8,128,64]{1,2,0:T(8,128)S(1)}, ...), condition=%wide.region_1.2_spmd.clone.clone, body=%wide.region_0.1_spmd.clone.clone.sunk | while | flops 42469380 | bytes 10887999 | solution.py:39
  50.9 1.3 constant_dynamic-slice_fusion.2
  52.2 0.7 copy.27
  52.9 2.9 copy.28
  55.8 1.4 compare_and_fusion.2
  57.2 1.9 gather_fusion
  59.1 1.2 fusion.47
  60.4 0.2 copy.29
  60.7 0.8 dynamic_slice.35
  61.4 0.3 fusion.49
  61.7 0.3 fusion.50
  62.1 1.3 constant_dynamic-slice_fusion.2
  63.4 0.7 copy.27
  64.1 2.9 copy.28
  67.0 1.4 compare_and_fusion.2
  68.4 1.9 gather_fusion
  70.3 1.2 fusion.47
  71.6 0.2 copy.29
  71.9 0.8 dynamic_slice.35
  72.6 0.3 fusion.49
  72.9 0.3 fusion.50
  73.2 0.1 bitcast_add_fusion.2
  73.3 0.2 copy.22
  73.5 0.9 convert_element_type.31
  74.5 143.2 %all-reduce.2.cloned.1.call-done = bf16[8,8192]{1,0:T(8,128)(2,1)} async-done(((bf16[8,8192]{1,0:T(8,128)(2,1)}), bf16[8,8192]{1,0:T(8,128)(2,1)}) %all-reduce.2.cloned.1.call-update) | async-done | bytes 131088 | tf_op jit(solution)/shard_map/psum | solution.py:41
  217.7 0.8 convolution_bitcast_fusion
  218.5 79.3 %psum.15 = f32[8,8]{0,1:T(8,128)S(1)} all-reduce(f32[8,8]{0,1:T(8,128)S(1)} %convolution_bitcast_fusion), channel_id=1, replica_groups=mesh['row'=32,'col'=8] {'row','col'}, use_global_device_ids=true, to_apply=%region_3.4 | all-reduce | flops 64 | bytes 512 | tf_op jit(solution)/shard_map/psum | solution.py:48
  297.8 1.3 fusion.19
  299.2 1.5 convolution_subtract_fusion
  (13 shorter events, 0.3 us)
Async XLA Ops:
  7.2 210.5 %all-reduce.2.cloned.1.call-start = ((), (), s32[]{:S(2)}) async-start(), calls=%async_computation | async-start | bytes 262144 | tf_op jit(solution)/shard_map/psum | solution.py:41
  50.8 166.9 %copy-start = (bf16[8,1024]{1,0:T(8,128)(2,1)S(1)}, bf16[8,1024]{1,0:T(8,128)(2,1)}, u32[]{:S(2)}) copy-start(bf16[8,1024]{1,0:T(8,128)(2,1)} %param.8) | copy-start | bytes 49156
  50.9 166.9 %copy-start.1 = (f32[1024]{0:T(1024)S(1)}, f32[1024]{0:T(1024)}, u32[]{:S(2)}) copy-start(f32[1024]{0:T(1024)} %param.9) | copy-start | bytes 12292
Sparse Core Ops, SparseCore 0:
  74.6 143.0 all-reduce.1
where the time goes:
time: 309 us; the launch traced here: 307 us
  waiting for transfers between devices  143 us (46%)
  blocking collectives  119 us (39%)
  local copies, waits for them, and re-layouts  19.5 us (6%)
  between operations  14.7 us (5%)
  matrix products  5.8 us (2%)
  other arithmetic  4.52 us (1%)
    psum x1, waiting for transfers between devices, per_device(): lax.psum(partial_value.astype(jnp.bfloat16), 'col').astype(jnp.float32)  143 us
    psum x1, blocking collectives, per_device(): gram = lax.psum(terms, ('row', 'col')) / total_states  79.3 us
    all_gather x1, blocking collectives, per_device(): gathered = lax.all_gather(vectors, 'row', axis=1, tiled=True)  40.2 us
  transfers between devices with their start and end apart: 1, of which 1 were waited for; matrix products, arithmetic and copies ran while one was open for 0% of the time, Pallas kernels for 0%

commit v1 on v0

--- a/solution.py
+++ b/solution.py
@@ -45,7 +45,7 @@
     whole = diag_part + share
     terms = jnp.einsum("an,bn->ab", vec32, whole, precision=lax.Precision.HIGHEST)
     total_states = n_row * n_col * own_states
-    gram = lax.psum(terms, ("row", "col")) / total_states
+    gram = jnp.sum(lax.all_gather(terms, ("row", "col")), axis=0) / total_states
     residual = whole - jnp.einsum("ab,an->bn", gram, vec32, precision=lax.Precision.HIGHEST)
     return (whole.astype(jnp.bfloat16), residual)
 

time: 309 us -> 860 us (2.78); the launches traced: 307 us -> 849 us
  blocking collectives: 119 us -> 661 us
    all_gather x0 -> x1, blocking collectives: none -> 621 us  [per_device(): gram = jnp.sum(lax.all_gather(terms, ('row', 'col')), axis=0) / total_states]
    psum x1 -> x0, blocking collectives: 79.3 us -> none  [per_device(): gram = lax.psum(terms, ('row', 'col')) / total_states]
where the time goes in v1:
time: 860 us; the launch traced here: 849 us
  blocking collectives  661 us (77%)
  waiting for transfers between devices  143 us (17%)
  local copies, waits for them, and re-layouts  19.7 us (2%)
  between operations  14.7 us (2%)
    all_gather x1, blocking collectives, per_device(): gram = jnp.sum(lax.all_gather(terms, ('row', 'col')), axis=0) / total_states  621 us
    psum x1, waiting for transfers between devices, per_device(): lax.psum(partial_value.astype(jnp.bfloat16), 'col').astype(jnp.float32)  143 us
    all_gather x1, blocking collectives, per_device(): gathered = lax.all_gather(vectors, 'row', axis=1, tiled=True)  40.2 us
  transfers between devices with their start and end apart: 1, of which 1 were waited for; matrix products, arithmetic and copies ran while one was open for 0% of the time, Pallas kernels for 0%

profile of v1, /device:TPU:1, one launch (start us, length us, event | category | flops | bytes accessed | tf_op | source)
XLA Modules:
  0.0 849.3 jit_solution(17125459617874427160)
XLA Ops:
  7.9 40.2 %all_gather.9 = bf16[8,32768]{1,0:T(8,128)(2,1)S(1)} all-gather(bf16[8,1024]{1,0:T(8,128)(2,1)} %param.8), channel_id=1, replica_groups=mesh['row'=32,'col'=8] {'row'}, dimensions={1}, use_global_device_ids=true | all-gather | bytes 540672 | tf_op jit(solution)/shard_map/all_gather | solution.py:16
  48.0 1.1 reshape.25
  49.2 1.7 copy.28
  50.9 22.4 %while.13 = (s32[]{:T(128)}, f32[8,128,64]{1,2,0:T(8,128)S(1)}, s32[]{:T(128)}, s32[1024]{0:T(1024)}, s32[]{:T(128)}, /*index=5*/s32[1024]{0:T(1024)}, bf16[8,51...) while((s32[]{:T(128)}, f32[8,128,64]{1,2,0:T(8,128)S(1)}, ...), condition=%wide.region_1.2_spmd.clone.clone, body=%wide.region_0.1_spmd.clone.clone.sunk | while | flops 42469380 | bytes 10887999 | solution.py:39
  50.9 1.3 constant_dynamic-slice_fusion.2
  52.2 0.7 copy.39
  52.9 2.9 copy.40
  55.8 1.4 compare_and_fusion.2
  57.2 1.9 gather_fusion
  59.1 1.2 fusion.47
  60.4 0.2 copy.41
  60.7 0.8 dynamic_slice.35
  61.4 0.3 fusion.49
  61.7 0.3 fusion.50
  62.1 1.3 constant_dynamic-slice_fusion.2
  63.4 0.7 copy.39
  64.1 2.9 copy.40
  67.0 1.4 compare_and_fusion.2
  68.4 1.9 gather_fusion
  70.3 1.2 fusion.47
  71.6 0.2 copy.41
  71.9 0.8 dynamic_slice.35
  72.6 0.3 fusion.49
  72.9 0.3 fusion.50
  73.3 0.2 copy.30
  73.5 0.9 convert_element_type.31
  74.5 143.2 %all-reduce.2.cloned.1.call-done = bf16[8,8192]{1,0:T(8,128)(2,1)} async-done(((bf16[8,8192]{1,0:T(8,128)(2,1)}), bf16[8,8192]{1,0:T(8,128)(2,1)}) %all-reduce.2.cloned.1.call-update) | async-done | bytes 131088 | tf_op jit(solution)/shard_map/psum | solution.py:41
  217.7 0.8 convolution_bitcast_fusion
  218.6 620.7 %all-gather = f32[2048,8]{1,0:T(8,128)S(1)} all-gather(f32[8,8]{1,0:T(8,128)S(1)} %copy.31), channel_id=2, replica_groups=mesh['row'=32,'col'=8] {'row','col'}, dimensions={0}, use_global_device_ids=true | all-gather | bytes 65792 | tf_op jit(solution)/shard_map/all_gather | solution.py:48
  839.3 0.3 bitcast_reduce_fusion
  839.7 1.3 fusion.19
  841.0 1.5 convolution_subtract_fusion
  (16 shorter events, 0.6 us)
Async XLA Ops:
  7.2 210.5 %all-reduce.2.cloned.1.call-start = ((), (), s32[]{:S(2)}) async-start(), calls=%async_computation | async-start | bytes 262144 | tf_op jit(solution)/shard_map/psum | solution.py:41
  50.8 166.9 %copy-start = (bf16[8,1024]{1,0:T(8,128)(2,1)S(1)}, bf16[8,1024]{1,0:T(8,128)(2,1)}, u32[]{:S(2)}) copy-start(bf16[8,1024]{1,0:T(8,128)(2,1)} %param.8) | copy-start | bytes 49156
  50.9 166.9 %copy-start.1 = (f32[1024]{0:T(1024)S(1)}, f32[1024]{0:T(1024)}, u32[]{:S(2)}) copy-start(f32[1024]{0:T(1024)} %param.9) | copy-start | bytes 12292
Sparse Core Ops, SparseCore 0:
  74.6 143.0 all-reduce.1
